TPU v7x, 32 devices: a whole 2x2x4 slice. The times are simulated.
32 devices in a mesh: near: 16 (over z, y, x), far: 2 (over core).
Axes of the slice: x: 2, y: 2, z: 4, core: 2. Of those that a mesh axis runs over, the one named last changes fastest.
Arguments:
- vectors: bfloat16 [128, 4, 480], P('near'), may hold values from -6 to 6
- near_blocks: bfloat16 [128, 16, 2, 240, 240], P('near', 'far'), may hold values from -0.09375 to 0.09375
- neighbours: int32 [128, 16], P('near', 'far'), may hold values from 0 to 127, as said below
- live_counts: int32 [128], P('near'), may hold values from 4 to 16, as said below
- tmatrix: float32 [128, 2, 240], P('near'), may hold values from -0.8 to 0.8
- agg_matrix: bfloat16 [480, 512], replicated, may hold values from -0.25 to 0.25
- sphere_box: int32 [128], P('near'), may hold values from 0 to 15, never falling along the last dimension, each value on 1 to 24 neighbouring positions
- agg_angle: float32 [128, 256], P('near'), may hold values from -3.140625 to 3.140625
- far_list: int32 [16, 16], P('far'), may hold values from 0 to 15, as said below
- far_factors: float32 [16, 16, 2, 256], P('far', None, None, 'near'), may hold values from -0.6 to 0.6
- dis_matrix: bfloat16 [512, 480], replicated, may hold values from -0.25 to 0.25
Outputs:
- first_image: bfloat16 [128, 4, 480], P('near')
- second_image: bfloat16 [128, 4, 480], P('near')
Inputs may be any that keep to these rules, and one draw needn't show every extreme that they name: `neighbours`: each entry differs from its row's sphere number by 1 to 8. `live_counts`: slots at or above a sphere's count are padding; some sphere has all 16 slots live. `sphere_box`: box numbers never fall along the spheres; every box holds 1 to 24 spheres. `far_list`: a box's far list names neither the box nor the boxes numbered one above or below it, counted around.
All inputs are finite; a program needn't handle non-finite values.
Results may differ from a plain program's by a relative error of at most 0.0052.
Values may be sent and summed in bfloat16 or wider, within the bound.
No kernel may reach another device: no remote copies, remote signals or barrier semaphores. Data moves between devices by JAX's collectives and lax.ppermute only.
A program may use at most 64 MiB of HBM per device.

v0:
```python
import jax
import jax.numpy as jnp
from jax import lax
from jax.sharding import PartitionSpec as P


def with_halo(block, sides, width):
    for axis, dim in sides:
        count = lax.axis_size(axis)
        forward = [(i, i + 1) for i in range(count - 1)]
        backward = [(target, source) for source, target in forward]
        low = lax.ppermute(
            lax.slice_in_dim(block, block.shape[dim] - width, None, axis=dim), axis, forward
        )
        high = lax.ppermute(lax.slice_in_dim(block, 0, width, axis=dim), axis, backward)
        block = jnp.concatenate([low, block, high], axis=dim)
    return block


def complex_mul(left_re, left_im, right_re, right_im):
    return (left_re * right_re - left_im * right_im, left_re * right_im + left_im * right_re)


def outgoing_of(rows_vec, cos_rows, sin_rows, agg_matrix):
    count, newton, width = rows_vec.shape
    waves = agg_matrix.shape[1] // 2
    product = jnp.dot(
        rows_vec.reshape(count * newton, width), agg_matrix, preferred_element_type=jnp.float32
    )
    product = product.reshape(count, newton, 2, waves)
    out_re, out_im = complex_mul(
        product[:, :, 0], product[:, :, 1], cos_rows[:, None, :], sin_rows[:, None, :]
    )
    return jnp.stack([out_re, out_im], axis=2)


def apply_operator(
    current,
    near_blocks,
    neighbours,
    live_counts,
    tmatrix,
    agg_matrix,
    sphere_box,
    agg_angle,
    far_list,
    far_factors,
    dis_matrix,
):
    sph_count, newton, width = current.shape
    coeffs = width // 2
    slots = neighbours.shape[1]
    own_boxes = far_list.shape[0]
    far_count = lax.axis_size("far")
    all_boxes = own_boxes * far_count
    waves = agg_matrix.shape[1] // 2
    near_pos = lax.axis_index("near")
    far_pos = lax.axis_index("far")
    padded = with_halo(current, (("near", 0),), sph_count)
    local_index = neighbours - (near_pos - 1) * sph_count
    gathered = padded[local_index]
    alive = (far_pos * slots + jnp.arange(slots, dtype=jnp.int32))[None, :] < live_counts[:, None]
    gathered = jnp.where(alive[:, :, None, None], gathered, jnp.zeros_like(gathered))
    both_parts = jnp.concatenate([gathered[..., :coeffs], gathered[..., coeffs:]], axis=2)
    with_real = jnp.einsum(
        "nkrc,nkcd->nrd", both_parts, near_blocks[:, :, 0], preferred_element_type=jnp.float32
    )
    with_imag = jnp.einsum(
        "nkrc,nkcd->nrd", both_parts, near_blocks[:, :, 1], preferred_element_type=jnp.float32
    )
    near_re = with_real[:, :newton] - with_imag[:, newton:]
    near_im = with_imag[:, :newton] + with_real[:, newton:]
    near_field = jnp.concatenate([near_re, near_im], axis=-1)
    cosine = jnp.cos(agg_angle)
    sine = jnp.sin(agg_angle)
    stacked = outgoing_of(current, cosine, sine, agg_matrix)
    member = (
        sphere_box[None, :] == far_pos * own_boxes + jnp.arange(own_boxes, dtype=jnp.int32)[:, None]
    ).astype(jnp.float32)
    partial_value = jnp.einsum("bn,nrtq->brtq", member, stacked, precision=lax.Precision.HIGHEST)
    box_waves = lax.psum_scatter(partial_value, "near", scatter_dimension=3, tiled=True)
    all_waves = lax.all_gather(box_waves, "far", axis=0, tiled=True)
    selector = (
        far_list[:, :, None] == jnp.arange(all_boxes, dtype=jnp.int32)[None, None, :]
    ).astype(jnp.float32)
    picked = jnp.einsum("gfb,brtq->gfrtq", selector, all_waves, precision=lax.Precision.HIGHEST)
    in_re, in_im = complex_mul(
        far_factors[:, :, None, 0, :],
        far_factors[:, :, None, 1, :],
        picked[:, :, :, 0],
        picked[:, :, :, 1],
    )
    incoming = jnp.stack([jnp.sum(in_re, axis=1), jnp.sum(in_im, axis=1)], axis=2)
    full_waves = lax.all_gather(incoming, "near", axis=3, tiled=True)
    owner = (
        sphere_box[:, None] == far_pos * own_boxes + jnp.arange(own_boxes, dtype=jnp.int32)[None, :]
    ).astype(jnp.float32)
    sphere_waves = jnp.einsum("nb,brtq->nrtq", owner, full_waves, precision=lax.Precision.HIGHEST)
    local_re, local_im = complex_mul(
        sphere_waves[:, :, 0], sphere_waves[:, :, 1], cosine[:, None, :], -sine[:, None, :]
    )
    local_waves = jnp.concatenate([local_re, local_im], axis=-1).astype(jnp.bfloat16)
    far_field = jnp.dot(
        local_waves.reshape(sph_count * newton, 2 * waves),
        dis_matrix,
        preferred_element_type=jnp.float32,
    )
    far_field = far_field.reshape(sph_count, newton, width)
    field = lax.psum(near_field + far_field, "far")
    scat_re, scat_im = complex_mul(
        tmatrix[:, None, 0, :], tmatrix[:, None, 1, :], field[..., :coeffs], field[..., coeffs:]
    )
    image = current.astype(jnp.float32) - jnp.concatenate([scat_re, scat_im], axis=-1)
    return image.astype(jnp.bfloat16)


def shards(
    vectors,
    near_blocks,
    neighbours,
    live_counts,
    tmatrix,
    agg_matrix,
    sphere_box,
    agg_angle,
    far_list,
    far_factors,
    dis_matrix,
):
    first_image = apply_operator(
        vectors,
        near_blocks,
        neighbours,
        live_counts,
        tmatrix,
        agg_matrix,
        sphere_box,
        agg_angle,
        far_list,
        far_factors,
        dis_matrix,
    )
    second_image = apply_operator(
        first_image,
        near_blocks,
        neighbours,
        live_counts,
        tmatrix,
        agg_matrix,
        sphere_box,
        agg_angle,
        far_list,
        far_factors,
        dis_matrix,
    )
    return (first_image, second_image)


def solution(mesh):
    return jax.shard_map(
        shards,
        mesh=mesh,
        in_specs=(
            P("near", None, None),
            P("near", "far", None, None, None),
            P("near", "far"),
            P("near"),
            P("near", None, None),
            P(),
            P("near"),
            P("near", None),
            P("far", None),
            P("far", None, None, "near"),
            P(),
        ),
        out_specs=(P("near", None, None), P("near", None, None)),
        check_vma=False,
    )
```

profile of v0, /device:TPU:0, one launch (start us, length us, event | category | flops | bytes accessed | tf_op | source)
XLA Modules:
  0.0 290.1 jit_solution(10729382742883723635)
XLA Ops:
  7.3 5.0 %collective-permute-start = (bf16[8,4,480]{2,1,0:T(4,128)(2,1)}, bf16[8,4,480]{2,1,0:T(4,128)(2,1)S(1)}, u32[]{:S(2)}, u32[]{:S(2)}) collective-permute-start(bf16[8,4,480]{2,1,0:T(4,128)(2,1)} %param.11), channel_id=1, source_target_pairs={{0,2},{2,4},{4,6},{6,8},{8,10},{10,12},{12,14},{14,16},{16,18},{18... | collective-permute-start | bytes 92168 | tf_op jit(solution)/shard_map/ppermute | solution.py:12
  12.3 1.3 collective-permute-start.1
  13.6 0.7 fusion.80
  14.4 1.2 fusion.29
  15.6 0.9 fusion.34
  16.5 0.7 copy.86
  17.2 1.9 reshape.112
  19.3 1.1 fusion.78
  20.4 0.7 broadcast_compare_fusion
  21.1 0.7 compare_select_fusion
  21.9 0.8 fusion.79
  22.7 0.8 pad_maximum_fusion.6
  23.6 0.8 gather_fusion
  24.4 0.2 broadcast_select_fusion.1
  24.6 0.1 fusion.77
  24.7 4.4 %fusion.12 = f32[8,8,240]{2,1,0:T(8,128)S(1)} fusion(bf16[8,8,2,240,240]{4,3,2,1,0:T(8,128)(2,1)} %param.12, bf16[8,8,4,240]{3,2,1,0:T(4,128)(2,1)S(1)} %get-tuple-element.9, bf16[8,8,4,240]{3,2,1,0:T(4,128)(2,1)S(1)} %get-tuple-element.8), kind=kOutput, calls=%fused_computation.14 | convolution fusion | flops 59473920 | bytes 8171520 | tf_op jit(solution)/shard_map/nkrc,nkcd->nrd/dot_general | solution.py:65
  29.2 4.4 %fusion.18 = f32[8,8,240]{2,1,0:T(8,128)S(1)} fusion(bf16[8,8,2,240,240]{4,3,2,1,0:T(8,128)(2,1)} %param.12, bf16[8,8,4,240]{3,2,1,0:T(4,128)(2,1)S(1)} %get-tuple-element.9, bf16[8,8,4,240]{3,2,1,0:T(4,128)(2,1)S(1)} %get-tuple-element.8), kind=kOutput, calls=%fused_computation.16 | convolution fusion | flops 59473920 | bytes 8171520 | tf_op jit(solution)/shard_map/nkrc,nkcd->nrd/dot_general | solution.py:68
  33.6 65.1 %reduce-scatter.7.cloned.1.call-done = f32[16,64]{1,0:T(8,128)} async-done(((f32[256,64]{1,0:T(8,128)}), f32[16,64]{1,0:T(8,128)}) %reduce-scatter.7.cloned.1.call-update) | async-done | bytes 4112
  98.7 0.8 reshape.113
  99.6 1.8 all_gather.12
  101.5 0.4 fusion.44
  101.9 0.2 subtract_reduce_fusion.1
  102.2 41.7 %all_gather.13 = f32[8,4,2,256]{0,1,2,3:T(4,128)S(1)} all-gather(f32[8,4,2,16]{0,1,2,3:T(4,128)S(1)} %copy.49), channel_id=1, replica_groups=mesh['near'=16,'far'=2] {'near'}, dimensions={3}, use_global_device_ids=true | all-gather | bytes 69632 | tf_op jit(solution)/shard_map/all_gather | solution.py:94
  143.9 0.7 fusion.26
  144.7 0.3 convolution_add_fusion.1
  144.9 3.6 %psum.14 = f32[8,4,480]{2,1,0:T(4,128)S(1)} all-reduce(f32[8,4,480]{2,1,0:T(4,128)S(1)} %convolution_add_fusion.1), channel_id=1, replica_groups=mesh['near'=16,'far'=2] {'far'}, use_global_device_ids=true, to_apply=%region_3.4 | all-reduce | flops 15360 | bytes 122880 | tf_op jit(solution)/shard_map/psum | solution.py:109
  148.7 4.0 %collective-permute-start.2 = (bf16[8,4,480]{2,1,0:T(4,128)(2,1)S(1)}, bf16[8,4,480]{2,1,0:T(4,128)(2,1)S(1)}, u32[]{:S(2)}, u32[]{:S(2)}) collective-permute-start(bf16[8,4,480]{2,1,0:T(4,128)(2,1)S(1)} %fusion.38), channel_id=1, source_target_pairs={{0,2},{2,4},{4,6},{6,8},{8,10},{10,12},{12,14},{14,16},{16,18},{18... | collective-permute-start | bytes 92168 | tf_op jit(solution)/shard_map/ppermute | solution.py:12
  152.8 1.3 collective-permute-start.3
  154.1 0.2 fusion.28
  154.3 0.2 fusion.39
  154.5 0.7 copy.88
  155.3 1.9 reshape.114
  157.3 1.3 collective-permute-done.3
  158.7 0.8 gather_fusion.1
  159.5 0.2 broadcast_select_fusion
  159.7 0.1 fusion.76
  159.8 4.4 %fusion.15 = f32[8,8,240]{2,1,0:T(8,128)S(1)} fusion(bf16[8,8,2,240,240]{4,3,2,1,0:T(8,128)(2,1)} %param.12, bf16[8,8,4,240]{3,2,1,0:T(4,128)(2,1)S(1)} %get-tuple-element.7, bf16[8,8,4,240]{3,2,1,0:T(4,128)(2,1)S(1)} %get-tuple-element.6), kind=kOutput, calls=%fused_computation.15 | convolution fusion | flops 59473920 | bytes 8171520 | tf_op jit(solution)/shard_map/nkrc,nkcd->nrd/dot_general | solution.py:65
  164.3 4.4 %fusion.21 = f32[8,8,240]{2,1,0:T(8,128)S(1)} fusion(bf16[8,8,2,240,240]{4,3,2,1,0:T(8,128)(2,1)} %param.12, bf16[8,8,4,240]{3,2,1,0:T(4,128)(2,1)S(1)} %get-tuple-element.7, bf16[8,8,4,240]{3,2,1,0:T(4,128)(2,1)S(1)} %get-tuple-element.6), kind=kOutput, calls=%fused_computation.17 | convolution fusion | flops 59473920 | bytes 8171520 | tf_op jit(solution)/shard_map/nkrc,nkcd->nrd/dot_general | solution.py:68
  168.7 64.0 %reduce-scatter.9.cloned.1.call-done = f32[16,64]{1,0:T(8,128)} async-done(((f32[256,64]{1,0:T(8,128)}), f32[16,64]{1,0:T(8,128)}) %reduce-scatter.9.cloned.1.call-update) | async-done | bytes 4112
  232.7 0.8 reshape.115
  233.6 1.8 all_gather.14
  235.4 0.4 fusion.46
  235.9 0.2 subtract_reduce_fusion
  236.2 41.7 %all_gather.15 = f32[8,4,2,256]{0,1,2,3:T(4,128)S(1)} all-gather(f32[8,4,2,16]{0,1,2,3:T(4,128)S(1)} %copy.58), channel_id=1, replica_groups=mesh['near'=16,'far'=2] {'near'}, dimensions={3}, use_global_device_ids=true | all-gather | bytes 69632 | tf_op jit(solution)/shard_map/all_gather | solution.py:94
  277.9 0.7 fusion.24
  278.6 0.3 convolution_add_fusion
  278.9 3.6 %psum.15 = f32[8,4,480]{2,1,0:T(4,128)S(1)} all-reduce(f32[8,4,480]{2,1,0:T(4,128)S(1)} %convolution_add_fusion), channel_id=1, replica_groups=mesh['near'=16,'far'=2] {'far'}, use_global_device_ids=true, to_apply=%region_7.8 | all-reduce | flops 15360 | bytes 122880 | tf_op jit(solution)/shard_map/psum | solution.py:109
  282.6 0.7 fusion.43
  (42 shorter events, 1.1 us)
Async XLA Ops:
  7.2 137.5 %copy-start = (bf16[512,480]{0,1:T(8,128)(2,1)S(1)}, bf16[512,480]{0,1:T(8,128)(2,1)}, u32[]{:S(2)}) copy-start(bf16[512,480]{0,1:T(8,128)(2,1)} %param.21) | copy-start | bytes 1474564
  7.2 141.4 %copy-start.3 = (bf16[8,4,480]{2,1,0:T(4,128)(2,1)S(1)}, bf16[8,4,480]{2,1,0:T(4,128)(2,1)}, u32[]{:S(2)}) copy-start(bf16[8,4,480]{2,1,0:T(4,128)(2,1)} %param.11) | copy-start | bytes 92164
  7.2 146.9 %copy-start.1 = (bf16[480,512]{1,0:T(8,128)(2,1)S(1)}, bf16[480,512]{1,0:T(8,128)(2,1)}, u32[]{:S(2)}) copy-start(bf16[480,512]{1,0:T(8,128)(2,1)} %param.16) | copy-start | bytes 1474564
  7.2 136.7 %copy-start.5 = (s32[8]{0:T(128)S(1)}, s32[8]{0:T(128)}, u32[]{:S(2)}) copy-start(s32[8]{0:T(128)} %param.17) | copy-start | bytes 100
  7.2 94.3 %copy-start.4 = (s32[8,16]{1,0:T(8,128)S(1)}, s32[8,16]{1,0:T(8,128)}, u32[]{:S(2)}) copy-start(s32[8,16]{1,0:T(8,128)} %param.19) | copy-start | bytes 1540
  7.2 91.5 %reduce-scatter.7.cloned.1.call-start = ((), (), s32[]{:S(2)}) async-start(), calls=%async_computation.2 | async-start | bytes 139264
  7.3 15.5 %collective-permute-start = (bf16[8,4,480]{2,1,0:T(4,128)(2,1)}, bf16[8,4,480]{2,1,0:T(4,128)(2,1)S(1)}, u32[]{:S(2)}, u32[]{:S(2)}) collective-permute-start(bf16[8,4,480]{2,1,0:T(4,128)(2,1)} %param.11), channel_id=1, source_target_pairs={{0,2},{2,4},{4,6},{6,8},{8,10},{10,12},{12,14},{14,16},{16,18},{18... | collective-permute-start | bytes 92168 | tf_op jit(solution)/shard_map/ppermute | solution.py:12
  12.3 10.5 %collective-permute-start.1 = (bf16[8,4,480]{2,1,0:T(4,128)(2,1)}, bf16[8,4,480]{2,1,0:T(4,128)(2,1)S(1)}, u32[]{:S(2)}, u32[]{:S(2)}) collective-permute-start(bf16[8,4,480]{2,1,0:T(4,128)(2,1)} %param.11), channel_id=1, source_target_pairs={{2,0},{4,2},{6,4},{8,6},{10,8},{12,10},{14,12},{16,14},{18,16},{20... | collective-permute-start | bytes 92168 | tf_op jit(solution)/shard_map/ppermute | solution.py:15
  19.2 213.5 %reduce-scatter.9.cloned.1.call-start = ((), (), s32[]{:S(2)}) async-start(), calls=%async_computation.3 | async-start | bytes 139264
  148.7 134.5 %copy-start.2 = (bf16[8,4,480]{2,1,0:T(4,128)(2,1)}, bf16[8,4,480]{2,1,0:T(4,128)(2,1)S(1)}, u32[]{:S(2)}) copy-start(bf16[8,4,480]{2,1,0:T(4,128)(2,1)S(1)} %fusion.38) | copy-start | bytes 92164
  148.7 8.5 %collective-permute-start.2 = (bf16[8,4,480]{2,1,0:T(4,128)(2,1)S(1)}, bf16[8,4,480]{2,1,0:T(4,128)(2,1)S(1)}, u32[]{:S(2)}, u32[]{:S(2)}) collective-permute-start(bf16[8,4,480]{2,1,0:T(4,128)(2,1)S(1)} %fusion.38), channel_id=1, source_target_pairs={{0,2},{2,4},{4,6},{6,8},{8,10},{10,12},{12,14},{14,16},{16,18},{18... | collective-permute-start | bytes 92168 | tf_op jit(solution)/shard_map/ppermute | solution.py:12
  152.8 5.8 %collective-permute-start.3 = (bf16[8,4,480]{2,1,0:T(4,128)(2,1)S(1)}, bf16[8,4,480]{2,1,0:T(4,128)(2,1)S(1)}, u32[]{:S(2)}, u32[]{:S(2)}) collective-permute-start(bf16[8,4,480]{2,1,0:T(4,128)(2,1)S(1)} %fusion.38), channel_id=1, source_target_pairs={{2,0},{4,2},{6,4},{8,6},{10,8},{12,10},{14,12},{16,14},{18,16},{20... | collective-permute-start | bytes 92168 | tf_op jit(solution)/shard_map/ppermute | solution.py:15
Sparse Core Ops, SparseCore 0:
  19.3 79.3 reduce-scatter.6
  157.4 75.2 reduce-scatter.8
where the time goes:
time: 291 us; the launch traced here: 290 us
  waiting for transfers between devices  130 us (45%)
  blocking collectives  94.3 us (32%)
  matrix products  22.9 us (8%)
  between operations  14.5 us (5%)
  local copies, waits for them, and re-layouts  12.1 us (4%)
  starting transfers between devices  11.7 us (4%)
  other arithmetic  4.22 us (1%)
    unnamed x4, waiting for transfers between devices  129 us
    all_gather x2, blocking collectives, apply_operator(): full_waves = lax.all_gather(incoming, 'near', axis=3, tiled=True)  83.4 us
    ppermute x2, starting transfers between devices, with_halo(): lax.ppermute(lax.slice_in_dim(block, block.shape[dim] - width, None, axis...  9.03 us
    dot_general x2, matrix products, apply_operator(): jnp.einsum('nkrc,nkcd->nrd', both_parts, near_blocks[:, :, 0], preferred_...  8.88 us
    dot_general x2, matrix products, apply_operator(): jnp.einsum('nkrc,nkcd->nrd', both_parts, near_blocks[:, :, 1], preferred_...  8.84 us
    unnamed x20, local copies, waits for them, and re-layouts  7.23 us
    psum x2, blocking collectives, apply_operator(): field = lax.psum(near_field + far_field, 'far')  7.18 us
  transfers between devices with their start and end apart: 6, of which 3 were waited for; matrix products, arithmetic and copies ran while one was open for 11% of the time, Pallas kernels for 0%

commit v1 on v0

--- a/solution.py
+++ b/solution.py
@@ -91,7 +91,24 @@
         picked[:, :, :, 1],
     )
     incoming = jnp.stack([jnp.sum(in_re, axis=1), jnp.sum(in_im, axis=1)], axis=2)
-    full_waves = lax.all_gather(incoming, "near", axis=3, tiled=True)
+    length, place, rows = (lax.axis_size("near"), lax.axis_index("near"), incoming.shape[3])
+    upward = [(i_2, (i_2 + 1) % length) for i_2 in range(length)]
+    left = [(i_2, (i_2 - 1) % length) for i_2 in range(length)]
+    out = jnp.zeros((*incoming.shape[:3], length * rows, *incoming.shape[3 + 1 :]), incoming.dtype)
+    out = lax.dynamic_update_slice_in_dim(out, incoming, place * rows, axis=3)
+    from_left = from_right = incoming
+    middle = length // 2
+    for step in range(1, middle + 1):
+        from_left = lax.ppermute(from_left, "near", upward)
+        out = lax.dynamic_update_slice_in_dim(
+            out, from_left, (place - step) % length * rows, axis=3
+        )
+        if step < length - middle:
+            from_right = lax.ppermute(from_right, "near", left)
+            out = lax.dynamic_update_slice_in_dim(
+                out, from_right, (place + step) % length * rows, axis=3
+            )
+    full_waves = out
     owner = (
         sphere_box[:, None] == far_pos * own_boxes + jnp.arange(own_boxes, dtype=jnp.int32)[None, :]
     ).astype(jnp.float32)

time: 291 us -> 359 us (1.23)
  blocking collectives: 94.3 us -> 11.1 us
  starting transfers between devices: 11.7 us -> 89.1 us
  local copies, waits for them, and re-layouts: 12.1 us -> 50.1 us
  waiting for transfers between devices: 130 us -> 166 us
    all_gather x2 -> x0, blocking collectives: 83.4 us -> none  [apply_operator(): full_waves = lax.all_gather(incoming, 'near', axis=3, tiled=True)]
    ppermute x0 -> x30, starting transfers between devices: none -> 80.1 us  [the longest x14 79.9 us: apply_operator(): from_right = lax.ppermute(from_right, 'near', left)]
    dynamic_update_slice x0 -> x32, local copies, waits for them, and re-layouts: none -> 38 us  [the longest x14 18.9 us: apply_operator(): lax.dynamic_update_slice_in_dim(out, from_right, (place + step) % length...]
    unnamed x4, waiting for transfers between devices: 129 us -> 152 us
    ppermute x0 -> x30, waiting for transfers between devices: none -> 14.3 us  [the longest x16 10.9 us: apply_operator(): from_left = lax.ppermute(from_left, 'near', upward)]
  transfers between devices with their start and end apart: 6 -> 36, of which waited for: 3 -> 16; matrix products, arithmetic and copies ran while one was open for 11% -> 20% of each run, Pallas kernels for 0% -> 0%
where the time goes in v1:
time: 359 us
  waiting for transfers between devices  166 us (46%)
  starting transfers between devices  89.1 us (25%)
  local copies, waits for them, and re-layouts  50.1 us (14%)
  matrix products  22.7 us (6%)
  between operations  15 us (4%)
  blocking collectives  11.1 us (3%)
  other arithmetic  4.18 us (1%)
    unnamed x4, waiting for transfers between devices  152 us
    ppermute x14, starting transfers between devices, apply_operator(): from_right = lax.ppermute(from_right, 'near', left)  79.9 us
    dynamic_update_slice x14, local copies, waits for them, and re-layouts, apply_operator(): lax.dynamic_update_slice_in_dim(out, from_right, (place + step) % length...  18.9 us
    dynamic_update_slice x16, local copies, waits for them, and re-layouts, apply_operator(): lax.dynamic_update_slice_in_dim(out, from_left, (place - step) % length *...  18.5 us
    ppermute x16, waiting for transfers between devices, apply_operator(): from_left = lax.ppermute(from_left, 'near', upward)  10.9 us
    dot_general x2, matrix products, apply_operator(): jnp.einsum('nkrc,nkcd->nrd', both_parts, near_blocks[:, :, 1], preferred_...  8.83 us
    dot_general x2, matrix products, apply_operator(): jnp.einsum('nkrc,nkcd->nrd', both_parts, near_blocks[:, :, 0], preferred_...  8.83 us
    psum x2, blocking collectives, apply_operator(): field = lax.psum(near_field + far_field, 'far')  7.36 us
  transfers between devices with their start and end apart: 36, of which 16 were waited for; matrix products, arithmetic and copies ran while one was open for 20% of the time, Pallas kernels for 0%

profile of v1, /device:TPU:0, one launch (start us, length us, event | category | flops | bytes accessed | tf_op | source)
XLA Modules:
  0.0 358.5 jit_solution(302043328521063693)
XLA Ops:
  7.2 5.0 %collective-permute-start = (bf16[8,4,480]{2,1,0:T(4,128)(2,1)}, bf16[8,4,480]{2,1,0:T(4,128)(2,1)S(1)}, u32[]{:S(2)}, u32[]{:S(2)}) collective-permute-start(bf16[8,4,480]{2,1,0:T(4,128)(2,1)} %param.11), channel_id=1, source_target_pairs={{0,2},{2,4},{4,6},{6,8},{8,10},{10,12},{12,14},{14,16},{16,18},{18... | collective-permute-start | bytes 92168 | tf_op jit(solution)/shard_map/ppermute | solution.py:12
  12.3 1.3 collective-permute-start.1
  17.3 1.9 reshape.112
  22.8 76.0 %reduce-scatter.7.cloned.1.call-done = f32[16,64]{1,0:T(8,128)} async-done(((f32[256,64]{1,0:T(8,128)}), f32[16,64]{1,0:T(8,128)}) %reduce-scatter.7.cloned.1.call-update) | async-done | bytes 4112
  99.7 1.8 all_gather.6
  103.0 5.5 %collective-permute-start.3 = (f32[8,4,2,16]{3,1,0,2:T(4,128)S(1)}, f32[8,4,2,16]{3,1,0,2:T(4,128)S(1)}, u32[]{:S(2)}, u32[]{:S(2)}) collective-permute-start(f32[8,4,2,16]{3,1,0,2:T(4,128)S(1)} %pad_maximum_fusion.8), channel_id=1, source_target_pairs={{0,30},{2,0},{4,2},{6,4},{8,6},{10,8},{12,10},{14,12},{16,14},{18,... | collective-permute-start | bytes 12296 | tf_op jit(solution)/shard_map/ppermute | solution.py:107
  108.5 1.9 collective-permute-done.2
  110.4 5.6 %collective-permute-start.5 = (f32[8,4,2,16]{3,1,0,2:T(4,128)S(1)}, f32[8,4,2,16]{3,1,0,2:T(4,128)S(1)}, u32[]{:S(2)}, u32[]{:S(2)}) collective-permute-start(f32[8,4,2,16]{3,1,0,2:T(4,128)S(1)} %collective-permute-done.3), channel_id=1, source_target_pairs={{0,30},{2,0},{4,2},{6,4},{8,6},{10,8},{12,10},{14,12},{16,14},{18,... | collective-permute-start | bytes 12296 | tf_op jit(solution)/shard_map/ppermute | solution.py:107
  116.0 1.9 collective-permute-done.4
  119.6 5.7 %collective-permute-start.7 = (f32[8,4,2,16]{3,1,0,2:T(4,128)S(1)}, f32[8,4,2,16]{3,1,0,2:T(4,128)S(1)}, u32[]{:S(2)}, u32[]{:S(2)}) collective-permute-start(f32[8,4,2,16]{3,1,0,2:T(4,128)S(1)} %collective-permute-done.5), channel_id=1, source_target_pairs={{0,30},{2,0},{4,2},{6,4},{8,6},{10,8},{12,10},{14,12},{16,14},{18,... | collective-permute-start | bytes 12296 | tf_op jit(solution)/shard_map/ppermute | solution.py:107
  126.8 5.9 %collective-permute-start.9 = (f32[8,4,2,16]{3,1,0,2:T(4,128)S(1)}, f32[8,4,2,16]{3,1,0,2:T(4,128)S(1)}, u32[]{:S(2)}, u32[]{:S(2)}) collective-permute-start(f32[8,4,2,16]{3,1,0,2:T(4,128)S(1)} %collective-permute-done.7), channel_id=1, source_target_pairs={{0,30},{2,0},{4,2},{6,4},{8,6},{10,8},{12,10},{14,12},{16,14},{18,... | collective-permute-start | bytes 12296 | tf_op jit(solution)/shard_map/ppermute | solution.py:107
  134.3 5.9 %collective-permute-start.11 = (f32[8,4,2,16]{3,1,0,2:T(4,128)S(1)}, f32[8,4,2,16]{3,1,0,2:T(4,128)S(1)}, u32[]{:S(2)}, u32[]{:S(2)}) collective-permute-start(f32[8,4,2,16]{3,1,0,2:T(4,128)S(1)} %collective-permute-done.9), channel_id=1, source_target_pairs={{0,30},{2,0},{4,2},{6,4},{8,6},{10,8},{12,10},{14,12},{16,14},{18,... | collective-permute-start | bytes 12296 | tf_op jit(solution)/shard_map/ppermute | solution.py:107
  140.5 4.4 %fusion.12 = f32[8,8,240]{2,1,0:T(8,128)S(1)} fusion(bf16[8,8,2,240,240]{4,3,2,1,0:T(8,128)(2,1)} %param.12, bf16[8,8,4,240]{3,2,1,0:T(4,128)(2,1)S(1)} %get-tuple-element.9, bf16[8,8,4,240]{3,2,1,0:T(4,128)(2,1)S(1)} %get-tuple-element.8), kind=kOutput, calls=%fused_computation.14 | convolution fusion | flops 59473920 | bytes 8171520 | tf_op jit(solution)/shard_map/nkrc,nkcd->nrd/dot_general | solution.py:65
  144.9 5.6 %collective-permute-start.13 = (f32[8,4,2,16]{3,1,0,2:T(4,128)S(1)}, f32[8,4,2,16]{3,1,0,2:T(4,128)S(1)}, u32[]{:S(2)}, u32[]{:S(2)}) collective-permute-start(f32[8,4,2,16]{3,1,0,2:T(4,128)S(1)} %collective-permute-done.11), channel_id=1, source_target_pairs={{0,30},{2,0},{4,2},{6,4},{8,6},{10,8},{12,10},{14,12},{16,14},{18,... | collective-permute-start | bytes 12296 | tf_op jit(solution)/shard_map/ppermute | solution.py:107
  150.5 4.4 %fusion.18 = f32[8,8,240]{2,1,0:T(8,128)S(1)} fusion(bf16[8,8,2,240,240]{4,3,2,1,0:T(8,128)(2,1)} %param.12, bf16[8,8,4,240]{3,2,1,0:T(4,128)(2,1)S(1)} %get-tuple-element.9, bf16[8,8,4,240]{3,2,1,0:T(4,128)(2,1)S(1)} %get-tuple-element.8), kind=kOutput, calls=%fused_computation.16 | convolution fusion | flops 59473920 | bytes 8171520 | tf_op jit(solution)/shard_map/nkrc,nkcd->nrd/dot_general | solution.py:68
  154.9 5.6 %collective-permute-start.15 = (f32[8,4,2,16]{3,1,0,2:T(4,128)S(1)}, f32[8,4,2,16]{3,1,0,2:T(4,128)S(1)}, u32[]{:S(2)}, u32[]{:S(2)}) collective-permute-start(f32[8,4,2,16]{3,1,0,2:T(4,128)S(1)} %collective-permute-done.13), channel_id=1, source_target_pairs={{0,30},{2,0},{4,2},{6,4},{8,6},{10,8},{12,10},{14,12},{16,14},{18,... | collective-permute-start | bytes 12296 | tf_op jit(solution)/shard_map/ppermute | solution.py:107
  162.3 1.4 dynamic_update_slice.98
  164.9 1.4 dynamic_update_slice.100
  167.6 1.4 dynamic_update_slice.102
  170.3 1.4 dynamic_update_slice.104
  173.0 1.4 dynamic_update_slice.106
  175.6 1.4 dynamic_update_slice.108
  178.3 1.4 dynamic_update_slice.110
  180.5 3.8 %psum.14 = f32[8,4,480]{2,1,0:T(4,128)S(1)} all-reduce(f32[8,4,480]{2,1,0:T(4,128)S(1)} %convolution_add_fusion.1), channel_id=1, replica_groups=mesh['near'=16,'far'=2] {'far'}, use_global_device_ids=true, to_apply=%region_3.4 | all-reduce | flops 15360 | bytes 122880 | tf_op jit(solution)/shard_map/psum | solution.py:126
  185.7 1.9 reshape.114
  187.7 1.3 collective-permute-start.17
  189.0 1.3 collective-permute-start.18
  190.3 75.9 %reduce-scatter.9.cloned.1.call-done = f32[16,64]{1,0:T(8,128)} async-done(((f32[256,64]{1,0:T(8,128)}), f32[16,64]{1,0:T(8,128)}) %reduce-scatter.9.cloned.1.call-update) | async-done | bytes 4112
  267.1 1.8 all_gather.7
  269.6 5.6 %collective-permute-start.20 = (f32[8,4,2,16]{3,1,0,2:T(4,128)S(1)}, f32[8,4,2,16]{3,1,0,2:T(4,128)S(1)}, u32[]{:S(2)}, u32[]{:S(2)}) collective-permute-start(f32[8,4,2,16]{3,1,0,2:T(4,128)S(1)} %pad_maximum_fusion.10), channel_id=1, source_target_pairs={{0,30},{2,0},{4,2},{6,4},{8,6},{10,8},{12,10},{14,12},{16,14},{18,... | collective-permute-start | bytes 12296 | tf_op jit(solution)/shard_map/ppermute | solution.py:107
  275.3 1.9 collective-permute-done.19
  277.1 5.6 %collective-permute-start.22 = (f32[8,4,2,16]{3,1,0,2:T(4,128)S(1)}, f32[8,4,2,16]{3,1,0,2:T(4,128)S(1)}, u32[]{:S(2)}, u32[]{:S(2)}) collective-permute-start(f32[8,4,2,16]{3,1,0,2:T(4,128)S(1)} %collective-permute-done.20), channel_id=1, source_target_pairs={{0,30},{2,0},{4,2},{6,4},{8,6},{10,8},{12,10},{14,12},{16,14},{18,... | collective-permute-start | bytes 12296 | tf_op jit(solution)/shard_map/ppermute | solution.py:107
  282.8 1.9 collective-permute-done.21
  285.6 5.7 %collective-permute-start.24 = (f32[8,4,2,16]{3,1,0,2:T(4,128)S(1)}, f32[8,4,2,16]{3,1,0,2:T(4,128)S(1)}, u32[]{:S(2)}, u32[]{:S(2)}) collective-permute-start(f32[8,4,2,16]{3,1,0,2:T(4,128)S(1)} %collective-permute-done.22), channel_id=1, source_target_pairs={{0,30},{2,0},{4,2},{6,4},{8,6},{10,8},{12,10},{14,12},{16,14},{18,... | collective-permute-start | bytes 12296 | tf_op jit(solution)/shard_map/ppermute | solution.py:107
  292.8 5.9 %collective-permute-start.26 = (f32[8,4,2,16]{3,1,0,2:T(4,128)S(1)}, f32[8,4,2,16]{3,1,0,2:T(4,128)S(1)}, u32[]{:S(2)}, u32[]{:S(2)}) collective-permute-start(f32[8,4,2,16]{3,1,0,2:T(4,128)S(1)} %collective-permute-done.24), channel_id=1, source_target_pairs={{0,30},{2,0},{4,2},{6,4},{8,6},{10,8},{12,10},{14,12},{16,14},{18,... | collective-permute-start | bytes 12296 | tf_op jit(solution)/shard_map/ppermute | solution.py:107
  300.4 5.9 %collective-permute-start.28 = (f32[8,4,2,16]{3,1,0,2:T(4,128)S(1)}, f32[8,4,2,16]{3,1,0,2:T(4,128)S(1)}, u32[]{:S(2)}, u32[]{:S(2)}) collective-permute-start(f32[8,4,2,16]{3,1,0,2:T(4,128)S(1)} %collective-permute-done.26), channel_id=1, source_target_pairs={{0,30},{2,0},{4,2},{6,4},{8,6},{10,8},{12,10},{14,12},{16,14},{18,... | collective-permute-start | bytes 12296 | tf_op jit(solution)/shard_map/ppermute | solution.py:107
  307.2 4.4 %fusion.15 = f32[8,8,240]{2,1,0:T(8,128)S(1)} fusion(bf16[8,8,2,240,240]{4,3,2,1,0:T(8,128)(2,1)} %param.12, bf16[8,8,4,240]{3,2,1,0:T(4,128)(2,1)S(1)} %get-tuple-element.7, bf16[8,8,4,240]{3,2,1,0:T(4,128)(2,1)S(1)} %get-tuple-element.6), kind=kOutput, calls=%fused_computation.15 | convolution fusion | flops 59473920 | bytes 8171520 | tf_op jit(solution)/shard_map/nkrc,nkcd->nrd/dot_general | solution.py:65
  311.6 5.6 %collective-permute-start.30 = (f32[8,4,2,16]{3,1,0,2:T(4,128)S(1)}, f32[8,4,2,16]{3,1,0,2:T(4,128)S(1)}, u32[]{:S(2)}, u32[]{:S(2)}) collective-permute-start(f32[8,4,2,16]{3,1,0,2:T(4,128)S(1)} %collective-permute-done.28), channel_id=1, source_target_pairs={{0,30},{2,0},{4,2},{6,4},{8,6},{10,8},{12,10},{14,12},{16,14},{18,... | collective-permute-start | bytes 12296 | tf_op jit(solution)/shard_map/ppermute | solution.py:107
  317.3 4.4 %fusion.21 = f32[8,8,240]{2,1,0:T(8,128)S(1)} fusion(bf16[8,8,2,240,240]{4,3,2,1,0:T(8,128)(2,1)} %param.12, bf16[8,8,4,240]{3,2,1,0:T(4,128)(2,1)S(1)} %get-tuple-element.7, bf16[8,8,4,240]{3,2,1,0:T(4,128)(2,1)S(1)} %get-tuple-element.6), kind=kOutput, calls=%fused_computation.17 | convolution fusion | flops 59473920 | bytes 8171520 | tf_op jit(solution)/shard_map/nkrc,nkcd->nrd/dot_general | solution.py:68
  321.7 5.6 %collective-permute-start.32 = (f32[8,4,2,16]{3,1,0,2:T(4,128)S(1)}, f32[8,4,2,16]{3,1,0,2:T(4,128)S(1)}, u32[]{:S(2)}, u32[]{:S(2)}) collective-permute-start(f32[8,4,2,16]{3,1,0,2:T(4,128)S(1)} %collective-permute-done.30), channel_id=1, source_target_pairs={{0,30},{2,0},{4,2},{6,4},{8,6},{10,8},{12,10},{14,12},{16,14},{18,... | collective-permute-start | bytes 12296 | tf_op jit(solution)/shard_map/ppermute | solution.py:107
  329.0 1.4 dynamic_update_slice.114
  331.7 1.4 dynamic_update_slice.116
  334.4 1.4 dynamic_update_slice.118
  337.0 1.4 dynamic_update_slice.120
  339.7 1.4 dynamic_update_slice.122
  342.4 1.4 dynamic_update_slice.124
  345.1 1.4 dynamic_update_slice.126
  347.3 3.6 %psum.15 = f32[8,4,480]{2,1,0:T(4,128)S(1)} all-reduce(f32[8,4,480]{2,1,0:T(4,128)S(1)} %convolution_add_fusion), channel_id=1, replica_groups=mesh['near'=16,'far'=2] {'far'}, use_global_device_ids=true, to_apply=%region_7.8 | all-reduce | flops 15360 | bytes 122880 | tf_op jit(solution)/shard_map/psum | solution.py:126
  (164 shorter events, 43.7 us)
Async XLA Ops:
  7.2 173.1 %copy-start = (bf16[512,480]{0,1:T(8,128)(2,1)S(1)}, bf16[512,480]{0,1:T(8,128)(2,1)}, u32[]{:S(2)}) copy-start(bf16[512,480]{0,1:T(8,128)(2,1)} %param.21) | copy-start | bytes 1474564
  7.2 172.8 %copy-start.5 = (s32[8]{0:T(128)S(1)}, s32[8]{0:T(128)}, u32[]{:S(2)}) copy-start(s32[8]{0:T(128)} %param.17) | copy-start | bytes 100
  7.2 91.6 %reduce-scatter.7.cloned.1.call-start = ((), (), s32[]{:S(2)}) async-start(), calls=%async_computation.2 | async-start | bytes 139264
  7.2 110.7 %collective-permute-start = (bf16[8,4,480]{2,1,0:T(4,128)(2,1)}, bf16[8,4,480]{2,1,0:T(4,128)(2,1)S(1)}, u32[]{:S(2)}, u32[]{:S(2)}) collective-permute-start(bf16[8,4,480]{2,1,0:T(4,128)(2,1)} %param.11), channel_id=1, source_target_pairs={{0,2},{2,4},{4,6},{6,8},{8,10},{10,12},{12,14},{14,16},{16,18},{18... | collective-permute-start | bytes 92168 | tf_op jit(solution)/shard_map/ppermute | solution.py:12
  12.3 105.7 %collective-permute-start.1 = (bf16[8,4,480]{2,1,0:T(4,128)(2,1)}, bf16[8,4,480]{2,1,0:T(4,128)(2,1)S(1)}, u32[]{:S(2)}, u32[]{:S(2)}) collective-permute-start(bf16[8,4,480]{2,1,0:T(4,128)(2,1)} %param.11), channel_id=1, source_target_pairs={{2,0},{4,2},{6,4},{8,6},{10,8},{12,10},{14,12},{16,14},{18,16},{20... | collective-permute-start | bytes 92168 | tf_op jit(solution)/shard_map/ppermute | solution.py:15
  14.3 170.1 %copy-start.3 = (bf16[8,4,480]{2,1,0:T(4,128)(2,1)S(1)}, bf16[8,4,480]{2,1,0:T(4,128)(2,1)}, u32[]{:S(2)}) copy-start(bf16[8,4,480]{2,1,0:T(4,128)(2,1)} %param.11) | copy-start | bytes 92164
  14.3 170.2 %copy-start.1 = (bf16[480,512]{1,0:T(8,128)(2,1)S(1)}, bf16[480,512]{1,0:T(8,128)(2,1)}, u32[]{:S(2)}) copy-start(bf16[480,512]{1,0:T(8,128)(2,1)} %param.16) | copy-start | bytes 1474564
  19.3 246.9 %reduce-scatter.9.cloned.1.call-start = ((), (), s32[]{:S(2)}) async-start(), calls=%async_computation.3 | async-start | bytes 139264
  22.8 246.2 %copy-start.4 = (s32[8,16]{1,0:T(8,128)S(1)}, s32[8,16]{1,0:T(8,128)}, u32[]{:S(2)}) copy-start(s32[8,16]{1,0:T(8,128)} %param.19) | copy-start | bytes 1540
  102.8 7.6 %collective-permute-start.2 = (f32[8,4,2,16]{3,1,0,2:T(4,128)S(1)}, f32[8,4,2,16]{3,1,0,2:T(4,128)S(1)}, u32[]{:S(2)}, u32[]{:S(2)}) collective-permute-start(f32[8,4,2,16]{3,1,0,2:T(4,128)S(1)} %pad_maximum_fusion.8), channel_id=1, source_target_pairs={{0,2},{2,4},{4,6},{6,8},{8,10},{10,12},{12,14},{14,16},{16,18},{18... | collective-permute-start | bytes 12296 | tf_op jit(solution)/shard_map/ppermute | solution.py:102
  103.0 7.4 %collective-permute-start.3 = (f32[8,4,2,16]{3,1,0,2:T(4,128)S(1)}, f32[8,4,2,16]{3,1,0,2:T(4,128)S(1)}, u32[]{:S(2)}, u32[]{:S(2)}) collective-permute-start(f32[8,4,2,16]{3,1,0,2:T(4,128)S(1)} %pad_maximum_fusion.8), channel_id=1, source_target_pairs={{0,30},{2,0},{4,2},{6,4},{8,6},{10,8},{12,10},{14,12},{16,14},{18,... | collective-permute-start | bytes 12296 | tf_op jit(solution)/shard_map/ppermute | solution.py:107
  110.4 7.5 %collective-permute-start.4 = (f32[8,4,2,16]{3,1,0,2:T(4,128)S(1)}, f32[8,4,2,16]{3,1,0,2:T(4,128)S(1)}, u32[]{:S(2)}, u32[]{:S(2)}) collective-permute-start(f32[8,4,2,16]{3,1,0,2:T(4,128)S(1)} %collective-permute-done.2), channel_id=1, source_target_pairs={{0,2},{2,4},{4,6},{6,8},{8,10},{10,12},{12,14},{14,16},{16,18},{18... | collective-permute-start | bytes 12296 | tf_op jit(solution)/shard_map/ppermute | solution.py:102
  110.4 9.2 %collective-permute-start.5 = (f32[8,4,2,16]{3,1,0,2:T(4,128)S(1)}, f32[8,4,2,16]{3,1,0,2:T(4,128)S(1)}, u32[]{:S(2)}, u32[]{:S(2)}) collective-permute-start(f32[8,4,2,16]{3,1,0,2:T(4,128)S(1)} %collective-permute-done.3), channel_id=1, source_target_pairs={{0,30},{2,0},{4,2},{6,4},{8,6},{10,8},{12,10},{14,12},{16,14},{18,... | collective-permute-start | bytes 12296 | tf_op jit(solution)/shard_map/ppermute | solution.py:107
  117.9 7.5 %collective-permute-start.6 = (f32[8,4,2,16]{3,1,0,2:T(4,128)S(1)}, f32[8,4,2,16]{3,1,0,2:T(4,128)S(1)}, u32[]{:S(2)}, u32[]{:S(2)}) collective-permute-start(f32[8,4,2,16]{3,1,0,2:T(4,128)S(1)} %collective-permute-done.4), channel_id=1, source_target_pairs={{0,2},{2,4},{4,6},{6,8},{8,10},{10,12},{12,14},{14,16},{16,18},{18... | collective-permute-start | bytes 12296 | tf_op jit(solution)/shard_map/ppermute | solution.py:102
  119.6 7.3 %collective-permute-start.7 = (f32[8,4,2,16]{3,1,0,2:T(4,128)S(1)}, f32[8,4,2,16]{3,1,0,2:T(4,128)S(1)}, u32[]{:S(2)}, u32[]{:S(2)}) collective-permute-start(f32[8,4,2,16]{3,1,0,2:T(4,128)S(1)} %collective-permute-done.5), channel_id=1, source_target_pairs={{0,30},{2,0},{4,2},{6,4},{8,6},{10,8},{12,10},{14,12},{16,14},{18,... | collective-permute-start | bytes 12296 | tf_op jit(solution)/shard_map/ppermute | solution.py:107
  125.4 7.5 %collective-permute-start.8 = (f32[8,4,2,16]{3,1,0,2:T(4,128)S(1)}, f32[8,4,2,16]{3,1,0,2:T(4,128)S(1)}, u32[]{:S(2)}, u32[]{:S(2)}) collective-permute-start(f32[8,4,2,16]{3,1,0,2:T(4,128)S(1)} %collective-permute-done.6), channel_id=1, source_target_pairs={{0,2},{2,4},{4,6},{6,8},{8,10},{10,12},{12,14},{14,16},{16,18},{18... | collective-permute-start | bytes 12296 | tf_op jit(solution)/shard_map/ppermute | solution.py:102
  126.8 7.5 %collective-permute-start.9 = (f32[8,4,2,16]{3,1,0,2:T(4,128)S(1)}, f32[8,4,2,16]{3,1,0,2:T(4,128)S(1)}, u32[]{:S(2)}, u32[]{:S(2)}) collective-permute-start(f32[8,4,2,16]{3,1,0,2:T(4,128)S(1)} %collective-permute-done.7), channel_id=1, source_target_pairs={{0,30},{2,0},{4,2},{6,4},{8,6},{10,8},{12,10},{14,12},{16,14},{18,... | collective-permute-start | bytes 12296 | tf_op jit(solution)/shard_map/ppermute | solution.py:107
  132.9 7.5 %collective-permute-start.10 = (f32[8,4,2,16]{3,1,0,2:T(4,128)S(1)}, f32[8,4,2,16]{3,1,0,2:T(4,128)S(1)}, u32[]{:S(2)}, u32[]{:S(2)}) collective-permute-start(f32[8,4,2,16]{3,1,0,2:T(4,128)S(1)} %collective-permute-done.8), channel_id=1, source_target_pairs={{0,2},{2,4},{4,6},{6,8},{8,10},{10,12},{12,14},{14,16},{16,18},{18... | collective-permute-start | bytes 12296 | tf_op jit(solution)/shard_map/ppermute | solution.py:102
  134.3 10.5 %collective-permute-start.11 = (f32[8,4,2,16]{3,1,0,2:T(4,128)S(1)}, f32[8,4,2,16]{3,1,0,2:T(4,128)S(1)}, u32[]{:S(2)}, u32[]{:S(2)}) collective-permute-start(f32[8,4,2,16]{3,1,0,2:T(4,128)S(1)} %collective-permute-done.9), channel_id=1, source_target_pairs={{0,30},{2,0},{4,2},{6,4},{8,6},{10,8},{12,10},{14,12},{16,14},{18,... | collective-permute-start | bytes 12296 | tf_op jit(solution)/shard_map/ppermute | solution.py:107
  140.5 10.1 %collective-permute-start.12 = (f32[8,4,2,16]{3,1,0,2:T(4,128)S(1)}, f32[8,4,2,16]{3,1,0,2:T(4,128)S(1)}, u32[]{:S(2)}, u32[]{:S(2)}) collective-permute-start(f32[8,4,2,16]{3,1,0,2:T(4,128)S(1)} %collective-permute-done.10), channel_id=1, source_target_pairs={{0,2},{2,4},{4,6},{6,8},{8,10},{10,12},{12,14},{14,16},{16,18},{18... | collective-permute-start | bytes 12296 | tf_op jit(solution)/shard_map/ppermute | solution.py:102
  144.9 10.1 %collective-permute-start.13 = (f32[8,4,2,16]{3,1,0,2:T(4,128)S(1)}, f32[8,4,2,16]{3,1,0,2:T(4,128)S(1)}, u32[]{:S(2)}, u32[]{:S(2)}) collective-permute-start(f32[8,4,2,16]{3,1,0,2:T(4,128)S(1)} %collective-permute-done.11), channel_id=1, source_target_pairs={{0,30},{2,0},{4,2},{6,4},{8,6},{10,8},{12,10},{14,12},{16,14},{18,... | collective-permute-start | bytes 12296 | tf_op jit(solution)/shard_map/ppermute | solution.py:107
  150.5 10.1 %collective-permute-start.14 = (f32[8,4,2,16]{3,1,0,2:T(4,128)S(1)}, f32[8,4,2,16]{3,1,0,2:T(4,128)S(1)}, u32[]{:S(2)}, u32[]{:S(2)}) collective-permute-start(f32[8,4,2,16]{3,1,0,2:T(4,128)S(1)} %collective-permute-done.12), channel_id=1, source_target_pairs={{0,2},{2,4},{4,6},{6,8},{8,10},{10,12},{12,14},{14,16},{16,18},{18... | collective-permute-start | bytes 12296 | tf_op jit(solution)/shard_map/ppermute | solution.py:102
  154.9 23.4 %collective-permute-start.15 = (f32[8,4,2,16]{3,1,0,2:T(4,128)S(1)}, f32[8,4,2,16]{3,1,0,2:T(4,128)S(1)}, u32[]{:S(2)}, u32[]{:S(2)}) collective-permute-start(f32[8,4,2,16]{3,1,0,2:T(4,128)S(1)} %collective-permute-done.13), channel_id=1, source_target_pairs={{0,30},{2,0},{4,2},{6,4},{8,6},{10,8},{12,10},{14,12},{16,14},{18,... | collective-permute-start | bytes 12296 | tf_op jit(solution)/shard_map/ppermute | solution.py:107
  160.6 19.1 %collective-permute-start.16 = (f32[8,4,2,16]{3,1,0,2:T(4,128)S(1)}, f32[8,4,2,16]{3,1,0,2:T(4,128)S(1)}, u32[]{:S(2)}, u32[]{:S(2)}) collective-permute-start(f32[8,4,2,16]{3,1,0,2:T(4,128)S(1)} %collective-permute-done.14), channel_id=1, source_target_pairs={{0,2},{2,4},{4,6},{6,8},{8,10},{10,12},{12,14},{14,16},{16,18},{18... | collective-permute-start | bytes 12296 | tf_op jit(solution)/shard_map/ppermute | solution.py:102
  184.5 167.1 %copy-start.2 = (bf16[8,4,480]{2,1,0:T(4,128)(2,1)}, bf16[8,4,480]{2,1,0:T(4,128)(2,1)S(1)}, u32[]{:S(2)}) copy-start(bf16[8,4,480]{2,1,0:T(4,128)(2,1)S(1)} %fusion.34) | copy-start | bytes 92164
  187.7 97.0 %collective-permute-start.17 = (bf16[8,4,480]{2,1,0:T(4,128)(2,1)S(1)}, bf16[8,4,480]{2,1,0:T(4,128)(2,1)S(1)}, u32[]{:S(2)}, u32[]{:S(2)}) collective-permute-start(bf16[8,4,480]{2,1,0:T(4,128)(2,1)S(1)} %fusion.34), channel_id=1, source_target_pairs={{0,2},{2,4},{4,6},{6,8},{8,10},{10,12},{12,14},{14,16},{16,18},{18... | collective-permute-start | bytes 92168 | tf_op jit(solution)/shard_map/ppermute | solution.py:12
  189.0 95.7 %collective-permute-start.18 = (bf16[8,4,480]{2,1,0:T(4,128)(2,1)S(1)}, bf16[8,4,480]{2,1,0:T(4,128)(2,1)S(1)}, u32[]{:S(2)}, u32[]{:S(2)}) collective-permute-start(bf16[8,4,480]{2,1,0:T(4,128)(2,1)S(1)} %fusion.34), channel_id=1, source_target_pairs={{2,0},{4,2},{6,4},{8,6},{10,8},{12,10},{14,12},{16,14},{18,16},{20... | collective-permute-start | bytes 92168 | tf_op jit(solution)/shard_map/ppermute | solution.py:15
  269.6 7.6 %collective-permute-start.19 = (f32[8,4,2,16]{3,1,0,2:T(4,128)S(1)}, f32[8,4,2,16]{3,1,0,2:T(4,128)S(1)}, u32[]{:S(2)}, u32[]{:S(2)}) collective-permute-start(f32[8,4,2,16]{3,1,0,2:T(4,128)S(1)} %pad_maximum_fusion.10), channel_id=1, source_target_pairs={{0,2},{2,4},{4,6},{6,8},{8,10},{10,12},{12,14},{14,16},{16,18},{18... | collective-permute-start | bytes 12296 | tf_op jit(solution)/shard_map/ppermute | solution.py:102
  269.6 7.5 %collective-permute-start.20 = (f32[8,4,2,16]{3,1,0,2:T(4,128)S(1)}, f32[8,4,2,16]{3,1,0,2:T(4,128)S(1)}, u32[]{:S(2)}, u32[]{:S(2)}) collective-permute-start(f32[8,4,2,16]{3,1,0,2:T(4,128)S(1)} %pad_maximum_fusion.10), channel_id=1, source_target_pairs={{0,30},{2,0},{4,2},{6,4},{8,6},{10,8},{12,10},{14,12},{16,14},{18,... | collective-permute-start | bytes 12296 | tf_op jit(solution)/shard_map/ppermute | solution.py:107
  277.1 7.5 %collective-permute-start.21 = (f32[8,4,2,16]{3,1,0,2:T(4,128)S(1)}, f32[8,4,2,16]{3,1,0,2:T(4,128)S(1)}, u32[]{:S(2)}, u32[]{:S(2)}) collective-permute-start(f32[8,4,2,16]{3,1,0,2:T(4,128)S(1)} %collective-permute-done.19), channel_id=1, source_target_pairs={{0,2},{2,4},{4,6},{6,8},{8,10},{10,12},{12,14},{14,16},{16,18},{18... | collective-permute-start | bytes 12296 | tf_op jit(solution)/shard_map/ppermute | solution.py:102
  277.1 8.4 %collective-permute-start.22 = (f32[8,4,2,16]{3,1,0,2:T(4,128)S(1)}, f32[8,4,2,16]{3,1,0,2:T(4,128)S(1)}, u32[]{:S(2)}, u32[]{:S(2)}) collective-permute-start(f32[8,4,2,16]{3,1,0,2:T(4,128)S(1)} %collective-permute-done.20), channel_id=1, source_target_pairs={{0,30},{2,0},{4,2},{6,4},{8,6},{10,8},{12,10},{14,12},{16,14},{18,... | collective-permute-start | bytes 12296 | tf_op jit(solution)/shard_map/ppermute | solution.py:107
  284.7 7.5 %collective-permute-start.23 = (f32[8,4,2,16]{3,1,0,2:T(4,128)S(1)}, f32[8,4,2,16]{3,1,0,2:T(4,128)S(1)}, u32[]{:S(2)}, u32[]{:S(2)}) collective-permute-start(f32[8,4,2,16]{3,1,0,2:T(4,128)S(1)} %collective-permute-done.21), channel_id=1, source_target_pairs={{0,2},{2,4},{4,6},{6,8},{8,10},{10,12},{12,14},{14,16},{16,18},{18... | collective-permute-start | bytes 12296 | tf_op jit(solution)/shard_map/ppermute | solution.py:102
  285.6 7.3 %collective-permute-start.24 = (f32[8,4,2,16]{3,1,0,2:T(4,128)S(1)}, f32[8,4,2,16]{3,1,0,2:T(4,128)S(1)}, u32[]{:S(2)}, u32[]{:S(2)}) collective-permute-start(f32[8,4,2,16]{3,1,0,2:T(4,128)S(1)} %collective-permute-done.22), channel_id=1, source_target_pairs={{0,30},{2,0},{4,2},{6,4},{8,6},{10,8},{12,10},{14,12},{16,14},{18,... | collective-permute-start | bytes 12296 | tf_op jit(solution)/shard_map/ppermute | solution.py:107
  292.2 7.5 %collective-permute-start.25 = (f32[8,4,2,16]{3,1,0,2:T(4,128)S(1)}, f32[8,4,2,16]{3,1,0,2:T(4,128)S(1)}, u32[]{:S(2)}, u32[]{:S(2)}) collective-permute-start(f32[8,4,2,16]{3,1,0,2:T(4,128)S(1)} %collective-permute-done.23), channel_id=1, source_target_pairs={{0,2},{2,4},{4,6},{6,8},{8,10},{10,12},{12,14},{14,16},{16,18},{18... | collective-permute-start | bytes 12296 | tf_op jit(solution)/shard_map/ppermute | solution.py:102
  292.8 7.5 %collective-permute-start.26 = (f32[8,4,2,16]{3,1,0,2:T(4,128)S(1)}, f32[8,4,2,16]{3,1,0,2:T(4,128)S(1)}, u32[]{:S(2)}, u32[]{:S(2)}) collective-permute-start(f32[8,4,2,16]{3,1,0,2:T(4,128)S(1)} %collective-permute-done.24), channel_id=1, source_target_pairs={{0,30},{2,0},{4,2},{6,4},{8,6},{10,8},{12,10},{14,12},{16,14},{18,... | collective-permute-start | bytes 12296 | tf_op jit(solution)/shard_map/ppermute | solution.py:107
  299.7 7.5 %collective-permute-start.27 = (f32[8,4,2,16]{3,1,0,2:T(4,128)S(1)}, f32[8,4,2,16]{3,1,0,2:T(4,128)S(1)}, u32[]{:S(2)}, u32[]{:S(2)}) collective-permute-start(f32[8,4,2,16]{3,1,0,2:T(4,128)S(1)} %collective-permute-done.25), channel_id=1, source_target_pairs={{0,2},{2,4},{4,6},{6,8},{8,10},{10,12},{12,14},{14,16},{16,18},{18... | collective-permute-start | bytes 12296 | tf_op jit(solution)/shard_map/ppermute | solution.py:102
  300.4 11.3 %collective-permute-start.28 = (f32[8,4,2,16]{3,1,0,2:T(4,128)S(1)}, f32[8,4,2,16]{3,1,0,2:T(4,128)S(1)}, u32[]{:S(2)}, u32[]{:S(2)}) collective-permute-start(f32[8,4,2,16]{3,1,0,2:T(4,128)S(1)} %collective-permute-done.26), channel_id=1, source_target_pairs={{0,30},{2,0},{4,2},{6,4},{8,6},{10,8},{12,10},{14,12},{16,14},{18,... | collective-permute-start | bytes 12296 | tf_op jit(solution)/shard_map/ppermute | solution.py:107
  307.2 10.1 %collective-permute-start.29 = (f32[8,4,2,16]{3,1,0,2:T(4,128)S(1)}, f32[8,4,2,16]{3,1,0,2:T(4,128)S(1)}, u32[]{:S(2)}, u32[]{:S(2)}) collective-permute-start(f32[8,4,2,16]{3,1,0,2:T(4,128)S(1)} %collective-permute-done.27), channel_id=1, source_target_pairs={{0,2},{2,4},{4,6},{6,8},{8,10},{10,12},{12,14},{14,16},{16,18},{18... | collective-permute-start | bytes 12296 | tf_op jit(solution)/shard_map/ppermute | solution.py:102
  311.6 10.1 %collective-permute-start.30 = (f32[8,4,2,16]{3,1,0,2:T(4,128)S(1)}, f32[8,4,2,16]{3,1,0,2:T(4,128)S(1)}, u32[]{:S(2)}, u32[]{:S(2)}) collective-permute-start(f32[8,4,2,16]{3,1,0,2:T(4,128)S(1)} %collective-permute-done.28), channel_id=1, source_target_pairs={{0,30},{2,0},{4,2},{6,4},{8,6},{10,8},{12,10},{14,12},{16,14},{18,... | collective-permute-start | bytes 12296 | tf_op jit(solution)/shard_map/ppermute | solution.py:107
  317.3 10.1 %collective-permute-start.31 = (f32[8,4,2,16]{3,1,0,2:T(4,128)S(1)}, f32[8,4,2,16]{3,1,0,2:T(4,128)S(1)}, u32[]{:S(2)}, u32[]{:S(2)}) collective-permute-start(f32[8,4,2,16]{3,1,0,2:T(4,128)S(1)} %collective-permute-done.29), channel_id=1, source_target_pairs={{0,2},{2,4},{4,6},{6,8},{8,10},{10,12},{12,14},{14,16},{16,18},{18... | collective-permute-start | bytes 12296 | tf_op jit(solution)/shard_map/ppermute | solution.py:102
  321.7 23.4 %collective-permute-start.32 = (f32[8,4,2,16]{3,1,0,2:T(4,128)S(1)}, f32[8,4,2,16]{3,1,0,2:T(4,128)S(1)}, u32[]{:S(2)}, u32[]{:S(2)}) collective-permute-start(f32[8,4,2,16]{3,1,0,2:T(4,128)S(1)} %collective-permute-done.30), channel_id=1, source_target_pairs={{0,30},{2,0},{4,2},{6,4},{8,6},{10,8},{12,10},{14,12},{16,14},{18,... | collective-permute-start | bytes 12296 | tf_op jit(solution)/shard_map/ppermute | solution.py:107
  327.3 19.1 %collective-permute-start.33 = (f32[8,4,2,16]{3,1,0,2:T(4,128)S(1)}, f32[8,4,2,16]{3,1,0,2:T(4,128)S(1)}, u32[]{:S(2)}, u32[]{:S(2)}) collective-permute-start(f32[8,4,2,16]{3,1,0,2:T(4,128)S(1)} %collective-permute-done.31), channel_id=1, source_target_pairs={{0,2},{2,4},{4,6},{6,8},{8,10},{10,12},{12,14},{14,16},{16,18},{18... | collective-permute-start | bytes 12296 | tf_op jit(solution)/shard_map/ppermute | solution.py:102
Sparse Core Ops, SparseCore 0:
  19.4 79.3 reduce-scatter.6
  187.8 78.3 reduce-scatter.8
